TPU v7x, 32 devices: a whole 2x2x4 slice. The times are simulated.
32 devices in a mesh: dp: 2 (over core), blk: 4 (over y, x), head: 4 (over z).
Axes of the slice: x: 2, y: 2, z: 4, core: 2. Of those that a mesh axis runs over, the one named last changes fastest.
Arguments:
- activations: bfloat16 [2, 2, 2048, 1536], P(None, 'dp', ('blk', 'head')), may hold values from -6 to 6
- segments: int32 [2, 2, 2048], P(None, 'dp', 'blk'), may hold values from 0 to 15, never falling along the last dimension, each value on 1 to 1024 neighbouring positions
- cotangent: bfloat16 [2, 2, 2048, 1536], P(None, 'dp', ('blk', 'head')), may hold values from -6 to 6
- norm_gain_one: bfloat16 [1536], P(('dp', 'blk')), may hold values from 0.5 to 1.5
- query_weight: bfloat16 [1536, 1536], P(('dp', 'blk')), may hold values from -0.15625 to 0.15625
- key_weight: bfloat16 [1536, 768], P(('dp', 'blk')), may hold values from -0.15625 to 0.15625
- value_weight: bfloat16 [1536, 768], P(('dp', 'blk')), may hold values from -0.15625 to 0.15625
- output_weight: bfloat16 [1536, 1536], P(('dp', 'blk')), may hold values from -1.25 to 1.25
- norm_gain_two: bfloat16 [1536], P(('dp', 'blk')), may hold values from 0.5 to 1.5
- gate_weight: bfloat16 [1536, 4096], P(('dp', 'blk')), may hold values from -0.15625 to 0.15625
- up_weight: bfloat16 [1536, 4096], P(('dp', 'blk')), may hold values from -0.15625 to 0.15625
- down_weight: bfloat16 [4096, 1536], P(('dp', 'blk')), may hold values from -0.09375 to 0.09375
Outputs:
- block_out: bfloat16 [2, 2, 2048, 1536], P(None, 'dp', ('blk', 'head'))
- grad_input: bfloat16 [2, 2, 2048, 1536], P(None, 'dp', ('blk', 'head'))
- grad_gain_one: float32 [1536], P(('dp', 'blk'))
- grad_query: float32 [1536, 1536], P(('dp', 'blk'))
- grad_key: float32 [1536, 768], P(('dp', 'blk'))
- grad_value: float32 [1536, 768], P(('dp', 'blk'))
- grad_output: float32 [1536, 1536], P(('dp', 'blk'))
- grad_gain_two: float32 [1536], P(('dp', 'blk'))
- grad_gate: float32 [1536, 4096], P(('dp', 'blk'))
- grad_up: float32 [1536, 4096], P(('dp', 'blk'))
- grad_down: float32 [4096, 1536], P(('dp', 'blk'))
Inputs may be any that keep to these rules, and one draw needn't show every extreme that they name: `segments`: along each sequence the segment numbers never fall and every number is used; a document has at most 1024 tokens, and in every sequence one has exactly that many.
All inputs are finite; a program needn't handle non-finite values.
Results may differ from a plain program's by a relative error of at most 0.023.
Values may be sent and summed in bfloat16 or wider, within the bound.
No kernel may reach another device: no remote copies, remote signals or barrier semaphores. Data moves between devices by JAX's collectives and lax.ppermute only.
A program may use at most 320 MiB of HBM per device.

v0:
```python
import math
import jax
import jax.numpy as jnp
from jax import lax
from jax.sharding import PartitionSpec as P

D = 1536
QH = 16
KVH = 8
HD = 96
FF = 4096
EPS = 1e-05
NEG = -1e30


def shortened(value):
    return jax.tree.map(lambda a: a.astype(jnp.bfloat16) if a.dtype == jnp.float32 else a, value)


def plain_dot(left, right):
    return jnp.dot(left, right, preferred_element_type=jnp.float32)


def first_dot(left, right):
    return lax.dot_general(
        left, right, (((0,), (0,)), ((), ())), preferred_element_type=jnp.float32
    )


def last_dot(left, right):
    return lax.dot_general(
        left, right, (((1,), (1,)), ((), ())), preferred_element_type=jnp.float32
    )


def normalize(values):
    factor = lax.rsqrt(jnp.mean(values * values, -1, keepdims=True) + EPS)
    return (values * factor, factor)


def norm_back(grad_norm, gain, normed, factor):
    scaled = grad_norm * gain
    return factor * (scaled - normed * jnp.mean(scaled * normed, -1, keepdims=True))


def per_device(
    activations,
    segments,
    cotangent,
    norm_gain_one,
    query_weight,
    key_weight,
    value_weight,
    output_weight,
    norm_gain_two,
    gate_weight,
    up_weight,
    down_weight,
):
    shards = (
        norm_gain_one,
        query_weight,
        key_weight,
        value_weight,
        output_weight,
        norm_gain_two,
        gate_weight,
        up_weight,
        down_weight,
    )
    head_count = lax.axis_size("head")
    cycle_count = lax.axis_size("blk")
    tok_rows = activations.shape[2]
    span_len = tok_rows * head_count
    seq_len = span_len * cycle_count
    heads_here = QH // head_count
    kv_repeat = max(1, head_count // KVH)
    kv_here = KVH * kv_repeat // head_count
    group_size = heads_here // kv_here
    block_rows = span_len if span_len <= 1024 else 1024
    block_count = span_len // block_rows
    scale = 1.0 / math.sqrt(HD)
    first_pos = lax.axis_index("blk") * span_len
    full_shapes = (
        (D,),
        (D, QH * HD),
        (D, KVH * HD),
        (D, KVH * HD),
        (QH * HD, D),
        (D,),
        (D, FF),
        (D, FF),
        (FF, D),
    )
    totals = tuple((jnp.zeros(shape_full, jnp.float32) for shape_full in full_shapes))
    results = []
    grads_x = []
    for batch_index in range(activations.shape[0]):
        seg_rows = segments[batch_index, 0]
        cot_rows = cotangent[batch_index, 0]
        gain_one = lax.all_gather(shards[0], ("dp", "blk"), axis=0, tiled=True)
        query_w = lax.all_gather(shards[1], ("dp", "blk"), axis=0, tiled=True)
        key_w = lax.all_gather(shards[2], ("dp", "blk"), axis=0, tiled=True)
        value_w = lax.all_gather(shards[3], ("dp", "blk"), axis=0, tiled=True)
        out_w = lax.all_gather(shards[4], ("dp", "blk"), axis=0, tiled=True)
        gain_two = lax.all_gather(shards[5], ("dp", "blk"), axis=0, tiled=True)
        gate_w = lax.all_gather(shards[6], ("dp", "blk"), axis=0, tiled=True)
        up_w = lax.all_gather(shards[7], ("dp", "blk"), axis=0, tiled=True)
        down_w = lax.all_gather(shards[8], ("dp", "blk"), axis=0, tiled=True)
        gain_one_f = gain_one.astype(jnp.float32)
        gain_two_f = gain_two.astype(jnp.float32)
        x_float = activations[batch_index, 0].astype(jnp.float32)
        normed_one, factor_one = normalize(x_float)
        input_one = (normed_one * gain_one_f).astype(jnp.bfloat16)
        queries = plain_dot(input_one, query_w).astype(jnp.bfloat16).reshape(tok_rows, QH, HD)
        keys = plain_dot(input_one, key_w).astype(jnp.bfloat16).reshape(tok_rows, KVH, HD)
        values = plain_dot(input_one, value_w).astype(jnp.bfloat16).reshape(tok_rows, KVH, HD)
        if kv_repeat > 1:
            keys = jnp.repeat(keys, kv_repeat, axis=1)
            values = jnp.repeat(values, kv_repeat, axis=1)
        head_q = lax.all_to_all(queries, "head", split_axis=1, concat_axis=0, tiled=True)
        head_k = lax.all_to_all(keys, "head", split_axis=1, concat_axis=0, tiled=True)
        head_v = lax.all_to_all(values, "head", split_axis=1, concat_axis=0, tiled=True)
        query_blocks = head_q.reshape(block_count, block_rows, kv_here, group_size, HD)
        pos_blocks = (first_pos + jnp.arange(span_len, dtype=jnp.int32)).reshape(
            block_count, block_rows
        )
        seg_blocks = seg_rows.reshape(block_count, block_rows)
        key_piece = lax.all_gather(head_k, "blk", axis=0, tiled=True)
        value_piece = lax.all_gather(head_v, "blk", axis=0, tiled=True)
        seg_piece = lax.all_gather(seg_rows, "blk", axis=0, tiled=True)
        key_pos = jnp.arange(key_piece.shape[0], dtype=jnp.int32)

        def one_block(inputs):
            query_blk, query_pos, query_seg, run_max, run_sum, run_acc = inputs
            scores = (
                jnp.einsum(
                    "qhrd,khd->hrqk", query_blk, key_piece, preferred_element_type=jnp.float32
                )
                * scale
            )
            allowed = (key_pos[None, :] <= query_pos[:, None]) & (
                seg_piece[None, :] == query_seg[:, None]
            )
            new_max = jnp.maximum(run_max, jnp.max(jnp.where(allowed, scores, NEG), axis=-1))
            expo = jnp.where(allowed, jnp.exp(scores - new_max[..., None]), 0.0)
            decay = jnp.exp(run_max - new_max)
            new_sum = run_sum * decay + jnp.sum(expo, -1)
            new_acc = run_acc * decay[..., None] + jnp.einsum(
                "hrqk,khd->hrqd",
                expo.astype(jnp.bfloat16),
                value_piece,
                preferred_element_type=jnp.float32,
            )
            return (new_max, new_sum, new_acc)

        run_max, run_sum, run_acc = lax.map(
            one_block,
            (
                query_blocks,
                pos_blocks,
                seg_blocks,
                jnp.full((block_count, kv_here, group_size, block_rows), NEG, jnp.float32),
                jnp.zeros((block_count, kv_here, group_size, block_rows), jnp.float32),
                jnp.zeros((block_count, kv_here, group_size, block_rows, HD), jnp.float32),
            ),
        )
        attn_heads = run_acc / run_sum[..., None]
        log_total = run_max + jnp.log(run_sum)
        attn_low = (
            attn_heads.transpose(0, 3, 1, 2, 4)
            .reshape(span_len, heads_here, HD)
            .astype(jnp.bfloat16)
        )
        attn_tok = lax.all_to_all(
            attn_low, "head", split_axis=0, concat_axis=1, tiled=True
        ).reshape(tok_rows, QH * HD)
        x_mid = x_float + plain_dot(attn_tok, out_w)
        normed_two, factor_two = normalize(x_mid)
        input_two = (normed_two * gain_two_f).astype(jnp.bfloat16)
        gate_val = plain_dot(input_two, gate_w)
        up_val = plain_dot(input_two, up_w)
        sigma = jax.nn.sigmoid(gate_val)
        silu_val = gate_val * sigma
        hidden = (silu_val * up_val).astype(jnp.bfloat16)
        result = (x_mid + plain_dot(hidden, down_w)).astype(jnp.bfloat16)
        grad_down = first_dot(hidden, cot_rows)
        grad_hidden = last_dot(cot_rows, down_w)
        grad_gate_val = (grad_hidden * up_val * sigma * (1.0 + gate_val * (1.0 - sigma))).astype(
            jnp.bfloat16
        )
        grad_up_val = (grad_hidden * silu_val).astype(jnp.bfloat16)
        grad_gate_w = first_dot(input_two, grad_gate_val)
        grad_up_w = first_dot(input_two, grad_up_val)
        grad_input_two = last_dot(grad_gate_val, gate_w) + last_dot(grad_up_val, up_w)
        grad_gain_two = jnp.sum(grad_input_two * normed_two, 0)
        grad_mid = cot_rows.astype(jnp.float32) + norm_back(
            grad_input_two, gain_two_f, normed_two, factor_two
        )
        grad_branch = grad_mid.astype(jnp.bfloat16)
        grad_out_w = first_dot(attn_tok, grad_branch)
        grad_attn = last_dot(grad_branch, out_w).astype(jnp.bfloat16).reshape(tok_rows, QH, HD)
        grad_heads = lax.all_to_all(grad_attn, "head", split_axis=1, concat_axis=0, tiled=True)
        grad_blocks = grad_heads.reshape(block_count, block_rows, kv_here, group_size, HD)
        delta = jnp.sum(grad_blocks.astype(jnp.float32).transpose(0, 2, 3, 1, 4) * attn_heads, -1)
        full_k = lax.all_gather(head_k, "blk", axis=0, tiled=True)
        full_v = lax.all_gather(head_v, "blk", axis=0, tiled=True)
        full_seg = lax.all_gather(seg_rows, "blk", axis=0, tiled=True)
        key_k = full_k.reshape(cycle_count, span_len, kv_here, HD)
        key_v = full_v.reshape(cycle_count, span_len, kv_here, HD)
        key_seg = full_seg.reshape(cycle_count, span_len)
        key_pos = jnp.arange(seq_len, dtype=jnp.int32).reshape(cycle_count, span_len)

        def key_step(grad_total, key_inputs):
            blk_k, blk_v, blk_seg, blk_pos = key_inputs

            def query_step(carry, inputs):
                sum_k, sum_v = carry
                query_blk, query_pos, query_seg, lse_blk, delta_blk, grad_blk = inputs
                scores = (
                    jnp.einsum(
                        "qhrd,khd->hrqk", query_blk, blk_k, preferred_element_type=jnp.float32
                    )
                    * scale
                )
                allowed = (blk_pos[None, :] <= query_pos[:, None]) & (
                    blk_seg[None, :] == query_seg[:, None]
                )
                probs = jnp.where(allowed, jnp.exp(scores - lse_blk[..., None]), 0.0)
                grad_probs = jnp.einsum(
                    "qhrd,khd->hrqk", grad_blk, blk_v, preferred_element_type=jnp.float32
                )
                grad_scores = (probs * (grad_probs - delta_blk[..., None])).astype(jnp.bfloat16)
                grad_query = (
                    jnp.einsum(
                        "hrqk,khd->qhrd", grad_scores, blk_k, preferred_element_type=jnp.float32
                    )
                    * scale
                )
                sum_k = (
                    sum_k
                    + jnp.einsum(
                        "hrqk,qhrd->khd", grad_scores, query_blk, preferred_element_type=jnp.float32
                    )
                    * scale
                )
                sum_v = sum_v + jnp.einsum(
                    "hrqk,qhrd->khd",
                    probs.astype(jnp.bfloat16),
                    grad_blk,
                    preferred_element_type=jnp.float32,
                )
                return ((sum_k, sum_v), grad_query)

            empty_kv = jnp.zeros((span_len, kv_here, HD), jnp.float32)
            (sum_k, sum_v), grad_part = lax.scan(
                query_step,
                (empty_kv, empty_kv),
                (query_blocks, pos_blocks, seg_blocks, log_total, delta, grad_blocks),
            )
            return (grad_total + grad_part, (sum_k, sum_v))

        grad_start = jnp.zeros((block_count, block_rows, kv_here, group_size, HD), jnp.float32)
        grad_query, (sums_k, sums_v) = lax.scan(
            key_step, grad_start, (key_k, key_v, key_seg, key_pos)
        )
        sum_k = sums_k.reshape(seq_len, kv_here, HD)
        sum_v = sums_v.reshape(seq_len, kv_here, HD)
        owned_k = lax.psum_scatter(
            sum_k.astype(jnp.bfloat16), "blk", scatter_dimension=0, tiled=True
        ).astype(jnp.float32)
        owned_v = lax.psum_scatter(
            sum_v.astype(jnp.bfloat16), "blk", scatter_dimension=0, tiled=True
        ).astype(jnp.float32)
        grad_query = grad_query.reshape(span_len, heads_here, HD)
        tok_q = lax.all_to_all(
            grad_query.astype(jnp.bfloat16), "head", split_axis=0, concat_axis=1, tiled=True
        ).astype(grad_query.dtype)
        tok_k = lax.all_to_all(
            owned_k.astype(jnp.bfloat16), "head", split_axis=0, concat_axis=1, tiled=True
        ).astype(owned_k.dtype)
        tok_v = lax.all_to_all(
            owned_v.astype(jnp.bfloat16), "head", split_axis=0, concat_axis=1, tiled=True
        ).astype(owned_v.dtype)
        tok_q = tok_q.reshape(tok_rows, QH * HD).astype(jnp.bfloat16)
        tok_k = (
            jnp.sum(tok_k.reshape(tok_rows, KVH, kv_repeat, HD), 2)
            .reshape(tok_rows, KVH * HD)
            .astype(jnp.bfloat16)
        )
        tok_v = (
            jnp.sum(tok_v.reshape(tok_rows, KVH, kv_repeat, HD), 2)
            .reshape(tok_rows, KVH * HD)
            .astype(jnp.bfloat16)
        )
        grad_query_w = first_dot(input_one, tok_q)
        grad_key_w = first_dot(input_one, tok_k)
        grad_value_w = first_dot(input_one, tok_v)
        grad_input_one = (
            last_dot(tok_q, query_w) + last_dot(tok_k, key_w) + last_dot(tok_v, value_w)
        )
        grad_gain_one = jnp.sum(grad_input_one * normed_one, 0)
        grad_x = (grad_mid + norm_back(grad_input_one, gain_one_f, normed_one, factor_one)).astype(
            jnp.bfloat16
        )
        result, grad_x, terms = (
            result,
            grad_x,
            (
                grad_gain_one,
                grad_query_w,
                grad_key_w,
                grad_value_w,
                grad_out_w,
                grad_gain_two,
                grad_gate_w,
                grad_up_w,
                grad_down,
            ),
        )
        results.append(result)
        grads_x.append(grad_x)
        totals = tuple((left + right for left, right in zip(totals, terms)))
    owned = jax.tree.map(
        lambda part: part.astype(jnp.float32),
        lax.psum_scatter(shortened(totals), ("dp", "blk"), scatter_dimension=0, tiled=True),
    )
    owned = jax.tree.map(lambda part: part.astype(jnp.float32), lax.psum(shortened(owned), "head"))
    block_out = jnp.stack(results)[:, None]
    grad_input = jnp.stack(grads_x)[:, None]
    return (
        block_out,
        grad_input,
        owned[0],
        owned[1],
        owned[2],
        owned[3],
        owned[4],
        owned[5],
        owned[6],
        owned[7],
        owned[8],
    )


def solution(mesh):
    placed = (
        P(None, "dp", ("blk", "head"), None),
        P(None, "dp", "blk"),
        P(None, "dp", ("blk", "head"), None),
        P(("dp", "blk")),
        P(("dp", "blk"), None),
        P(("dp", "blk"), None),
        P(("dp", "blk"), None),
        P(("dp", "blk"), None),
        P(("dp", "blk")),
        P(("dp", "blk"), None),
        P(("dp", "blk"), None),
        P(("dp", "blk"), None),
    )
    return jax.shard_map(
        per_device,
        mesh=mesh,
        in_specs=placed,
        out_specs=(
            P(None, "dp", ("blk", "head"), None),
            P(None, "dp", ("blk", "head"), None),
            P(("dp", "blk")),
            P(("dp", "blk"), None),
            P(("dp", "blk"), None),
            P(("dp", "blk"), None),
            P(("dp", "blk"), None),
            P(("dp", "blk")),
            P(("dp", "blk"), None),
            P(("dp", "blk"), None),
            P(("dp", "blk"), None),
        ),
        check_vma=False,
    )
```

profile of v0, /device:TPU:0, one launch (start us, length us, event | category | flops | bytes accessed | tf_op | source)
XLA Modules:
  0.0 1429.7 jit_solution(12849763053035598999)
XLA Ops:
  13.7 16.3 %all-reduce.5 = (bf16[1536]{0:T(1024)(128)(2,1)S(1)}, bf16[1536]{0:T(1024)(128)(2,1)S(1)}) all-reduce(bf16[1536]{0:T(1024)(128)(2,1)S(1)} %dynamic-update-slice, bf16[1536]{0:T(1024)(128)(2,1)S(1)} %dynamic-update-slice.1), channel_id=1, replica_groups=mesh['dp'=2,'blk'=4,'head'=4] {'dp','blk'}, use_global_device_ids=true, to_apply=%add | all-reduce | flops 3072 | bytes 12288
  57.7 15.3 %all-gather.14.cloned.1.call-done = bf16[1536,768]{1,0:T(8,128)(2,1)} async-done(((bf16[192,768]{1,0:T(8,128)(2,1)}), bf16[1536,768]{1,0:T(8,128)(2,1)}) %all-gather.14.cloned.1.call-update) | async-done | bytes 2359312 | tf_op jit(solution)/shard_map/all_gather | solution.py:104
  105.3 13.9 all_gather.73
  119.2 14.7 %all_gather.74 = bf16[2048,2,96]{0,2,1:T(8,128)(2,1)} all-gather(bf16[512,2,96]{0,2,1:T(8,128)(2,1)S(1)} %all_to_all.220), channel_id=1, replica_groups=mesh['dp'=2,'blk'=4,'head'=4] {'blk'}, dimensions={0}, use_global_device_ids=true | all-gather | bytes 983040 | tf_op jit(solution)/shard_map/all_gather | solution.py:130
  144.3 20.2 %all_gather.63 = bf16[2048,2,96]{0,2,1:T(8,128)(2,1)} all-gather(bf16[512,2,96]{0,2,1:T(8,128)(2,1)S(1)} %all_to_all.199), channel_id=1, replica_groups=mesh['dp'=2,'blk'=4,'head'=4] {'blk'}, dimensions={0}, use_global_device_ids=true | all-gather | bytes 983040 | tf_op jit(solution)/shard_map/all_gather | solution.py:129
  164.8 11.4 all_gather.66
  258.6 55.3 %all-gather.20.cloned.1.call-done = bf16[1536,4096]{1,0:T(8,128)(2,1)} async-done(((bf16[192,4096]{1,0:T(8,128)(2,1)}), bf16[1536,4096]{1,0:T(8,128)(2,1)}) %all-gather.20.cloned.1.call-update) | async-done | bytes 12582928 | tf_op jit(solution)/shard_map/all_gather | solution.py:108
  321.6 66.3 %all-gather.22.cloned.1.call-done = bf16[4096,1536]{1,0:T(8,128)(2,1)} async-done(((bf16[512,1536]{1,0:T(8,128)(2,1)}), bf16[4096,1536]{1,0:T(8,128)(2,1)}) %all-gather.22.cloned.1.call-update) | async-done | bytes 12582928 | tf_op jit(solution)/shard_map/all_gather | solution.py:109
  387.9 11.4 multiply_convert_fusion.2
  399.4 10.5 fusion.214
  409.9 11.6 multiply_reduce_fusion.1
  432.2 9.9 multiply_convert_fusion
  489.3 50.1 %while.25 = (s32[]{:T(128)}, f32[1,512,2,2,96]{1,4,3,2,0:T(8,128)}, bf16[4,512,2,96]{1,3,2,0:T(8,128)(2,1)}, bf16[4,512,2,96]{1,3,2,0:T(8,128)(2,1)}, bf16[4,512...) while((s32[]{:T(128)}, f32[1,512,2,2,96]{1,4,3,2,0:T(8,128)}, ...), condition=%wide.region_18.19_spmd.clone, body=%wide.region_17.18_spmd.clone.sunk | while | flops 1018593792 | bytes 67217776 | solution.py:264
  545.2 46.2 %while.24 = (s32[]{:T(128)}, f32[1,512,2,2,96]{1,4,3,2,0:T(8,128)S(1)}, bf16[4,512,2,96]{1,3,2,0:T(8,128)(2,1)}, bf16[4,512,2,96]{1,3,2,0:T(8,128)(2,1)}, bf16[4...) while((s32[]{:T(128)}, ...), condition=%wide.region_11.12_spmd.clone, body=%wide.region_10.11_spmd.clone.sunk | while | flops 1018593792 | bytes 69314976 | solution.py:264
  604.0 16.3 %reduce-scatter.12.cloned.1.call-done = bf16[512,2,96]{0,2,1:T(8,128)(2,1)} async-done(((bf16[2048,2,96]{0,2,1:T(8,128)(2,1)}), bf16[512,2,96]{0,2,1:T(8,128)(2,1)}) %reduce-scatter.12.cloned.1.call-update) | async-done | bytes 196624 | tf_op jit(solution)/shard_map/reduce_scatter | solution.py:269
  639.1 10.6 reduce-scatter.18.cloned.1.call-done
  656.2 22.6 %reduce-scatter.14.cloned.1.call-done = bf16[512,2,96]{0,2,1:T(8,128)(2,1)} async-done(((bf16[2048,2,96]{0,2,1:T(8,128)(2,1)}), bf16[512,2,96]{0,2,1:T(8,128)(2,1)}) %reduce-scatter.14.cloned.1.call-update) | async-done | bytes 196624 | tf_op jit(solution)/shard_map/reduce_scatter | solution.py:272
  710.1 11.7 all-to-all-done.13
  725.7 12.8 all-to-all-done.9
  745.0 11.8 fusion.218
  756.8 14.7 %add_convert_fusion.2 = bf16[1536,4096]{1,0:T(8,128)(2,1)} fusion(f32[1536,4096]{1,0:T(8,128)} %fusion.218, bf16[128,1536]{1,0:T(8,128)(2,1)S(1)} %copy-done.16, bf16[128,4096]{1,0:T(8,128)(2,1)S(1)} %copy-done.37), kind=kOutput, calls=%fused_computation.80 | convolution fusion | flops 1623195648 | bytes 39190528 | tf_op jit(solution)/shard_map/dot_general | solution.py:25
  771.7 12.2 fusion.219
  783.9 16.2 %add_convert_fusion.1 = bf16[1536,4096]{1,0:T(8,128)(2,1)} fusion(f32[1536,4096]{1,0:T(8,128)} %fusion.219, bf16[128,1536]{1,0:T(8,128)(2,1)S(1)} %copy-done.16, bf16[128,4096]{1,0:T(8,128)(2,1)S(1)} %copy-done.35), kind=kOutput, calls=%fused_computation.79 | convolution fusion | flops 1623195648 | bytes 39190528 | tf_op jit(solution)/shard_map/dot_general | solution.py:25
  801.2 11.9 fusion.165
  813.2 15.4 %add_convert_fusion = bf16[4096,1536]{1,0:T(8,128)(2,1)} fusion(f32[4096,1536]{1,0:T(8,128)} %fusion.165, bf16[128,4096]{1,0:T(8,128)(2,1)S(1)} %copy-done.25, bf16[2,1,128,1536]{3,2,1,0:T(8,128)(2,1)S(1)} %copy-done.45), kind=kOutput, calls=%fused_computation.78 | convolution fusion | flops 1623195648 | bytes 39190528 | tf_op jit(solution)/shard_map/dot_general | solution.py:25
  829.1 57.6 %reduce-scatter.20.cloned.1.call-done = bf16[192,1536]{1,0:T(8,128)(2,1)} async-done(((bf16[1536,1536]{1,0:T(8,128)(2,1)}), bf16[192,1536]{1,0:T(8,128)(2,1)}) %reduce-scatter.20.cloned.1.call-update) | async-done | bytes 589840 | tf_op jit(solution)/shard_map/reduce_scatter | solution.py:326
  886.7 95.8 %reduce-scatter.28.cloned.1.call-done = bf16[192,4096]{1,0:T(8,128)(2,1)} async-done(((bf16[1536,4096]{1,0:T(8,128)(2,1)}), bf16[192,4096]{1,0:T(8,128)(2,1)}) %reduce-scatter.28.cloned.1.call-update) | async-done | bytes 1572880 | tf_op jit(solution)/shard_map/reduce_scatter | solution.py:326
  982.4 95.8 %reduce-scatter.30.cloned.1.call-done = bf16[192,4096]{1,0:T(8,128)(2,1)} async-done(((bf16[1536,4096]{1,0:T(8,128)(2,1)}), bf16[192,4096]{1,0:T(8,128)(2,1)}) %reduce-scatter.30.cloned.1.call-update) | async-done | bytes 1572880 | tf_op jit(solution)/shard_map/reduce_scatter | solution.py:326
  1078.2 95.8 %reduce-scatter.32.cloned.1.call-done = bf16[512,1536]{1,0:T(8,128)(2,1)} async-done(((bf16[4096,1536]{1,0:T(8,128)(2,1)}), bf16[512,1536]{1,0:T(8,128)(2,1)}) %reduce-scatter.32.cloned.1.call-update) | async-done | bytes 1572880 | tf_op jit(solution)/shard_map/reduce_scatter | solution.py:326
  1198.1 14.9 %all-reduce.4 = (bf16[1536]{0:T(1024)(128)(2,1)S(1)}, bf16[1536]{0:T(1024)(128)(2,1)S(1)}) all-reduce(bf16[1536]{0:T(1024)(128)(2,1)S(1)} %add_convert_fusion.6, bf16[1536]{0:T(1024)(128)(2,1)S(1)} %add_convert_fusion.5), channel_id=8, replica_groups=mesh['dp'=2,'blk'=4,'head'=4] {'dp','blk'}, use_global_device_ids=true, to_apply=%region_24.25.clone | all-reduce | flops 3072 | bytes 12288
  1213.2 12.1 all-reduce.6
  1229.1 179.4 %all-reduce.10.cloned.1.call-done = (bf16[192,1536]{1,0:T(8,128)(2,1)}, bf16[192,768]{1,0:T(8,128)(2,1)}, bf16[192,768]{1,0:T(8,128)(2,1)}, bf16[192,1536]{1,0:T...) async-done(((bf16[192,1536]{1,0:T(8,128)(2,1)}, bf16[192,768]{1,0:T(8,128)(2,1)}, bf16[192,768]{1,0:T(8,128)(2,1)}, ...) | async-done | bytes 6488080 | tf_op jit(solution)/shard_map/psum | solution.py:328
  (567 shorter events, 446.9 us)
Async XLA Ops:
  7.2 42.5 %all-gather.10.cloned.1.call-start = ((), (), s32[]{:S(2)}) async-start(), calls=%async_computation.27 | async-start | bytes 2654208 | tf_op jit(solution)/shard_map/all_gather | solution.py:103
  8.0 65.1 %all-gather.14.cloned.1.call-start = ((), (), s32[]{:S(2)}) async-start(), calls=%async_computation.29 | async-start | bytes 2654208 | tf_op jit(solution)/shard_map/all_gather | solution.py:104
  8.7 125.2 %all-gather.12.cloned.1.call-start = ((), (), s32[]{:S(2)}) async-start(), calls=%async_computation.28 | async-start | bytes 5308416 | tf_op jit(solution)/shard_map/all_gather | solution.py:102
  9.5 234.9 %all-gather.16.cloned.1.call-start = ((), (), s32[]{:S(2)}) async-start(), calls=%async_computation.30 | async-start | bytes 5308416 | tf_op jit(solution)/shard_map/all_gather | solution.py:105
  10.0 240.1 %all-gather.18.cloned.1.call-start = ((), (), s32[]{:S(2)}) async-start(), calls=%async_computation.31 | async-start | bytes 14155776 | tf_op jit(solution)/shard_map/all_gather | solution.py:107
  10.6 303.3 %all-gather.20.cloned.1.call-start = ((), (), s32[]{:S(2)}) async-start(), calls=%async_computation.32 | async-start | bytes 14155776 | tf_op jit(solution)/shard_map/all_gather | solution.py:108
  11.2 376.8 %all-gather.22.cloned.1.call-start = ((), (), s32[]{:S(2)}) async-start(), calls=%async_computation.33 | async-start | bytes 14155776 | tf_op jit(solution)/shard_map/all_gather | solution.py:109
  52.8 25.0 %all-to-all-start.4 = ((bf16[128,8,96]{0,2,1:T(8,128)(2,1)}), bf16[128,8,96]{0,2,1:T(8,128)(2,1)S(1)}, u32[]{:S(2)}, u32[]{:S(2)}) async-start(bf16[128,8,96]{0,2,1:T(8,128)(2,1)} %bitcast.29), calls=%async_computation.4 | async-start | bytes 393216 | tf_op jit(solution)/shard_map/all_to_all | solution.py:122
  100.8 37.3 %all-to-all-start.2 = ((bf16[128,8,96]{0,2,1:T(8,128)(2,1)}), bf16[128,8,96]{0,2,1:T(8,128)(2,1)S(1)}, u32[]{:S(2)}, u32[]{:S(2)}) async-start(bf16[128,8,96]{0,2,1:T(8,128)(2,1)} %bitcast.13), calls=%async_computation.2 | async-start | bytes 393216 | tf_op jit(solution)/shard_map/all_to_all | solution.py:123
  138.0 44.7 %all-to-all-start.5 = ((bf16[128,16,96]{0,2,1:T(8,128)(2,1)}), bf16[128,16,96]{0,2,1:T(8,128)(2,1)S(1)}, u32[]{:S(2)}, u32[]{:S(2)}) async-start(bf16[128,16,96]{0,2,1:T(8,128)(2,1)} %bitcast.34), calls=%async_computation.5 | async-start | bytes 786432 | tf_op jit(solution)/shard_map/all_to_all | solution.py:121
  182.7 22.0 %all-to-all-start.1 = ((bf16[128,16,96]{0,2,1:T(8,128)(2,1)}), bf16[128,16,96]{0,2,1:T(8,128)(2,1)}, u32[]{:S(2)}, u32[]{:S(2)}) async-start(bf16[128,16,96]{0,2,1:T(8,128)(2,1)} %bitcast.9), calls=%async_computation.1 | async-start | bytes 786432 | tf_op jit(solution)/shard_map/all_to_all | solution.py:121
  204.7 22.1 %all-to-all-start.7 = ((bf16[512,4,96]{2,1,0:T(4,128)(2,1)}), bf16[512,4,96]{2,1,0:T(4,128)(2,1)S(1)}, u32[]{:S(2)}, u32[]{:S(2)}) async-start(bf16[512,4,96]{2,1,0:T(4,128)(2,1)} %copy.196), calls=%async_computation.7 | async-start | bytes 1048576 | tf_op jit(solution)/shard_map/all_to_all | solution.py:175
  226.8 16.0 %all-to-all-start.3 = ((bf16[512,4,96]{2,1,0:T(4,128)(2,1)}), bf16[512,4,96]{2,1,0:T(4,128)(2,1)}, u32[]{:S(2)}, u32[]{:S(2)}) async-start(bf16[512,4,96]{2,1,0:T(4,128)(2,1)} %copy.186), calls=%async_computation.3 | async-start | bytes 1048576 | tf_op jit(solution)/shard_map/all_to_all | solution.py:175
  464.8 16.7 %all-to-all-start.12 = ((bf16[128,16,96]{0,2,1:T(8,128)(2,1)}), bf16[128,16,96]{0,2,1:T(8,128)(2,1)S(1)}, u32[]{:S(2)}, u32[]{:S(2)}) async-start(bf16[128,16,96]{0,2,1:T(8,128)(2,1)} %bitcast.78), calls=%async_computation.14 | async-start | bytes 786432 | tf_op jit(solution)/shard_map/all_to_all | solution.py:203
  481.5 60.2 %all-to-all-start.8 = ((bf16[128,16,96]{0,2,1:T(8,128)(2,1)}), bf16[128,16,96]{0,2,1:T(8,128)(2,1)}, u32[]{:S(2)}, u32[]{:S(2)}) async-start(bf16[128,16,96]{0,2,1:T(8,128)(2,1)} %bitcast.57), calls=%async_computation.8 | async-start | bytes 786432 | tf_op jit(solution)/shard_map/all_to_all | solution.py:203
  485.6 111.4 %reduce-scatter.16.cloned.1.call-start = ((), (), s32[]{:S(2)}) async-start(), calls=%async_computation.36 | async-start | bytes 983040 | tf_op jit(solution)/shard_map/reduce_scatter | solution.py:269
  541.7 78.7 %reduce-scatter.12.cloned.1.call-start = ((), (), s32[]{:S(2)}) async-start(), calls=%async_computation.34 | async-start | bytes 983040 | tf_op jit(solution)/shard_map/reduce_scatter | solution.py:269
  593.7 56.1 %reduce-scatter.18.cloned.1.call-start = ((), (), s32[]{:S(2)}) async-start(), calls=%async_computation.37 | async-start | bytes 983040 | tf_op jit(solution)/shard_map/reduce_scatter | solution.py:272
  596.0 82.8 %reduce-scatter.14.cloned.1.call-start = ((), (), s32[]{:S(2)}) async-start(), calls=%async_computation.35 | async-start | bytes 983040 | tf_op jit(solution)/shard_map/reduce_scatter | solution.py:272
  598.9 23.3 %all-to-all-start.14 = ((bf16[512,2,96]{2,1,0:T(2,128)(2,1)}), bf16[512,2,96]{2,1,0:T(2,128)(2,1)S(1)}, u32[]{:S(2)}, u32[]{:S(2)}) async-start(bf16[512,2,96]{2,1,0:T(2,128)(2,1)} %copy.222), calls=%async_computation.17 | async-start | bytes 524288 | tf_op jit(solution)/shard_map/all_to_all | solution.py:279
  622.2 13.5 all-to-all-start.10
  626.7 202.2 %reduce-scatter.22.cloned.1.call-start = ((), (), s32[]{:S(2)}) async-start(), calls=%async_computation.39 | async-start | bytes 2654208 | tf_op jit(solution)/shard_map/reduce_scatter | solution.py:326
  651.6 29.0 %all-to-all-start.15 = ((bf16[512,2,96]{2,1,0:T(2,128)(2,1)}), bf16[512,2,96]{2,1,0:T(2,128)(2,1)S(1)}, u32[]{:S(2)}, u32[]{:S(2)}) async-start(bf16[512,2,96]{2,1,0:T(2,128)(2,1)} %copy.226), calls=%async_computation.19 | async-start | bytes 524288 | tf_op jit(solution)/shard_map/all_to_all | solution.py:282
  685.2 143.8 %reduce-scatter.24.cloned.1.call-start = ((), (), s32[]{:S(2)}) async-start(), calls=%async_computation.40 | async-start | bytes 2654208 | tf_op jit(solution)/shard_map/reduce_scatter | solution.py:326
  697.6 131.5 %reduce-scatter.26.cloned.1.call-start = ((), (), s32[]{:S(2)}) async-start(), calls=%async_computation.41 | async-start | bytes 5308416 | tf_op jit(solution)/shard_map/reduce_scatter | solution.py:326
  705.5 16.4 %all-to-all-start.13 = ((bf16[512,4,96]{2,1,0:T(4,128)(2,1)}), bf16[512,4,96]{2,1,0:T(4,128)(2,1)S(1)}, u32[]{:S(2)}, u32[]{:S(2)}) async-start(bf16[512,4,96]{2,1,0:T(4,128)(2,1)} %bitcast.83), calls=%async_computation.15 | async-start | bytes 1048576 | tf_op jit(solution)/shard_map/all_to_all | solution.py:276
  721.9 16.6 %all-to-all-start.9 = ((bf16[512,4,96]{2,1,0:T(4,128)(2,1)}), bf16[512,4,96]{2,1,0:T(4,128)(2,1)S(1)}, u32[]{:S(2)}, u32[]{:S(2)}) async-start(bf16[512,4,96]{2,1,0:T(4,128)(2,1)} %bitcast.62), calls=%async_computation.9 | async-start | bytes 1048576 | tf_op jit(solution)/shard_map/all_to_all | solution.py:276
  725.4 161.3 %reduce-scatter.20.cloned.1.call-start = ((), (), s32[]{:S(2)}) async-start(), calls=%async_computation.38 | async-start | bytes 5308416 | tf_op jit(solution)/shard_map/reduce_scatter | solution.py:326
  744.0 238.4 %reduce-scatter.28.cloned.1.call-start = ((), (), s32[]{:S(2)}) async-start(), calls=%async_computation.42 | async-start | bytes 14155776 | tf_op jit(solution)/shard_map/reduce_scatter | solution.py:326
  771.5 306.7 %reduce-scatter.30.cloned.1.call-start = ((), (), s32[]{:S(2)}) async-start(), calls=%async_computation.43 | async-start | bytes 14155776 | tf_op jit(solution)/shard_map/reduce_scatter | solution.py:326
  800.1 373.9 %reduce-scatter.32.cloned.1.call-start = ((), (), s32[]{:S(2)}) async-start(), calls=%async_computation.44 | async-start | bytes 14155776 | tf_op jit(solution)/shard_map/reduce_scatter | solution.py:326
  828.7 579.8 %all-reduce.10.cloned.1.call-start = ((), (), s32[]{:S(2)}) async-start(), calls=%async_computation.45 | async-start | bytes 12976128 | tf_op jit(solution)/shard_map/psum | solution.py:328
  (139 other events, 2642.1 us)
Sparse Core Ops, SparseCore 0:
  9.9 32.1 all-gather.9
  44.0 28.9 all-gather.13
  75.0 42.0 all-gather.11
  118.8 46.9 all-gather.15
  167.5 72.4 all-gather.17
  241.7 72.1 all-gather.19
  315.8 72.1 all-gather.21
  541.8 26.5 reduce-scatter.15
  593.8 26.4 reduce-scatter.11
  623.7 26.0 reduce-scatter.17
  652.7 26.0 reduce-scatter.13
  682.6 42.4 reduce-scatter.21
  729.4 42.4 reduce-scatter.23
  775.2 53.8 reduce-scatter.25
  832.8 53.8 reduce-scatter.19
  890.0 92.3 reduce-scatter.27
  985.8 92.3 reduce-scatter.29
  1081.6 92.3 reduce-scatter.31
  1176.9 231.5 all-reduce.9
where the time goes:
time: 1440 us; the launch traced here: 1430 us
  waiting for transfers between devices  770 us (53%)
  matrix products  342 us (24%)
  blocking collectives  119 us (8%)
  starting transfers between devices  74.8 us (5%)
  local copies, waits for them, and re-layouts  70.3 us (5%)
  other arithmetic  35.4 us (2%)
  between operations  16.9 us (1%)
    reduce_scatter x7, waiting for transfers between devices, per_device(): lax.psum_scatter(shortened(totals), ('dp', 'blk'), scatter_dimension=0, t...  345 us
    psum x1, waiting for transfers between devices, per_device(): lax.psum(shortened(owned), 'head')  179 us
    dot_general x14, matrix products, first_dot(): lax.dot_general(left, right, (((0,), (0,)), ((), ())), preferred_element_...  98.8 us
    dot_general x14, matrix products, last_dot(): lax.dot_general(left, right, (((1,), (1,)), ((), ())), preferred_element_...  76.6 us
    all_gather x1, waiting for transfers between devices, per_device(): down_w = lax.all_gather(shards[8], ('dp', 'blk'), axis=0, tiled=True)  66.3 us
    dot_general x14, matrix products, plain_dot(): return jnp.dot(left, right, preferred_element_type=jnp.float32)  63.4 us
    all_gather x1, waiting for transfers between devices, per_device(): up_w = lax.all_gather(shards[7], ('dp', 'blk'), axis=0, tiled=True)  55.3 us
    all_gather x2, blocking collectives, per_device(): key_piece = lax.all_gather(head_k, 'blk', axis=0, tiled=True)  34.2 us
  transfers between devices with their start and end apart: 35, of which 19 were waited for; matrix products, arithmetic and copies ran while one was open for 24% of the time, Pallas kernels for 0%

commit v1 on v0

--- a/solution.py
+++ b/solution.py
@@ -1,3 +1,4 @@
+import functools
 import math
 import jax
 import jax.numpy as jnp
@@ -11,6 +12,35 @@
 FF = 4096
 EPS = 1e-05
 NEG = -1e30
+
+
+def drive_ticks_over_axis(target, array_dim):
+    y = list(target.shape[1:])
+    y[array_dim] *= target.shape[0]
+    base_arr = jnp.moveaxis(target, 0, array_dim).reshape(y)
+    return base_arr
+
+
+def map_see(local_block, named_axis, d0):
+    k_all = jax.lax.axis_size(named_axis)
+    shelf = tuple(((i, (i + 1) % k_all) for i in range(k_all)))
+    then, piece_out = ([], [])
+    pile = tuple(((pp, dev_j) for dev_j, pp in shelf))
+    for tick in range(k_all - 1):
+        if tick % 2 == 0:
+            then.append(jax.lax.ppermute(then[-1] if then else local_block, named_axis, shelf))
+        else:
+            piece_out.append(
+                jax.lax.ppermute(piece_out[-1] if piece_out else local_block, named_axis, pile)
+            )
+    piece_now = jnp.stack([*then[::-1], local_block, *piece_out])
+    arr_now = jax.lax.axis_index(named_axis) - len(then)
+    piece_now = piece_now[(jnp.arange(k_all) - arr_now) % k_all]
+    y2 = drive_ticks_over_axis(piece_now, d0)
+    return y2
+
+
+test_sides = functools.partial(map_see, named_axis=("dp", "blk"), d0=0)
 
 
 def shortened(value):
@@ -106,7 +136,7 @@
         gain_two = lax.all_gather(shards[5], ("dp", "blk"), axis=0, tiled=True)
         gate_w = lax.all_gather(shards[6], ("dp", "blk"), axis=0, tiled=True)
         up_w = lax.all_gather(shards[7], ("dp", "blk"), axis=0, tiled=True)
-        down_w = lax.all_gather(shards[8], ("dp", "blk"), axis=0, tiled=True)
+        down_w = test_sides(shards[8])
         gain_one_f = gain_one.astype(jnp.float32)
         gain_two_f = gain_two.astype(jnp.float32)
         x_float = activations[batch_index, 0].astype(jnp.float32)

time: 1440 us -> 1630 us (1.13)
  blocking collectives: 119 us -> 321 us
  waiting for transfers between devices: 770 us -> 726 us
  local copies, waits for them, and re-layouts: 70.3 us -> 110 us
  matrix products: 342 us -> 324 us
    all_gather x2, blocking collectives: 15.8 us -> 111 us  [per_device(): seg_piece = lax.all_gather(seg_rows, 'blk', axis=0, tiled=True)]
    ppermute x0 -> x7, waiting for transfers between devices: none -> 90.2 us  [the longest x4 90.2 us: map_see(): jax.lax.ppermute(then[-1] if then else local_block, named_axis, shelf)]
    all_gather x1 -> x0, waiting for transfers between devices: 66.3 us -> none  [per_device(): down_w = lax.all_gather(shards[8], ('dp', 'blk'), axis=0, tiled=True)]
    all_gather x2, blocking collectives: 34.2 us -> 99.5 us  [per_device(): key_piece = lax.all_gather(head_k, 'blk', axis=0, tiled=True)]
    all_gather x1, waiting for transfers between devices: 55.3 us -> 0.01 us  [per_device(): up_w = lax.all_gather(shards[7], ('dp', 'blk'), axis=0, tiled=True)]
    unnamed x2, blocking collectives: 31.2 us -> 70.2 us
    unnamed x167 -> x184, local copies, waits for them, and re-layouts: 5.38 us -> 25.2 us
  transfers between devices with their start and end apart: 35 -> 41, of which waited for: 19 -> 21; matrix products, arithmetic and copies ran while one was open for 24% -> 22% of each run, Pallas kernels for 0% -> 0%
where the time goes in v1:
time: 1630 us; the launch traced here: 1620 us
  waiting for transfers between devices  726 us (45%)
  matrix products  324 us (20%)
  blocking collectives  321 us (20%)
  local copies, waits for them, and re-layouts  110 us (7%)
  starting transfers between devices  82.5 us (5%)
  other arithmetic  39.5 us (2%)
  between operations  17.5 us (1%)
    reduce_scatter x7, waiting for transfers between devices, per_device(): lax.psum_scatter(shortened(totals), ('dp', 'blk'), scatter_dimension=0, t...  345 us
    psum x1, waiting for transfers between devices, per_device(): lax.psum(shortened(owned), 'head')  179 us
    all_gather x2, blocking collectives, per_device(): seg_piece = lax.all_gather(seg_rows, 'blk', axis=0, tiled=True)  111 us
    all_gather x2, blocking collectives, per_device(): key_piece = lax.all_gather(head_k, 'blk', axis=0, tiled=True)  99.5 us
    dot_general x14, matrix products, first_dot(): lax.dot_general(left, right, (((0,), (0,)), ((), ())), preferred_element_...  98.8 us
    ppermute x4, waiting for transfers between devices, map_see(): jax.lax.ppermute(then[-1] if then else local_block, named_axis, shelf)  90.2 us
    unnamed x2, blocking collectives  70.2 us
    dot_general x14, matrix products, last_dot(): lax.dot_general(left, right, (((1,), (1,)), ((), ())), preferred_element_...  64.2 us
  transfers between devices with their start and end apart: 41, of which 21 were waited for; matrix products, arithmetic and copies ran while one was open for 22% of the time, Pallas kernels for 0%

profile of v1, /device:TPU:0, one launch (start us, length us, event | category | flops | bytes accessed | tf_op | source)
XLA Modules:
  0.0 1621.0 jit_solution(9110955388017164264)
XLA Ops:
  13.7 44.3 %collective-permute-done = bf16[512,1536]{1,0:T(8,128)(2,1)} collective-permute-done((bf16[512,1536]{1,0:T(8,128)(2,1)}, bf16[512,1536]{1,0:T(8,128)(2,1)}, u32[]{:S(2)}, u32[]{:S(2)}) %collective-permute-start) | collective-permute-done | bytes 1572896 | tf_op jit(solution)/shard_map/ppermute | solution.py:31
  60.6 45.9 %collective-permute-done.1 = bf16[512,1536]{1,0:T(8,128)(2,1)} collective-permute-done((bf16[512,1536]{1,0:T(8,128)(2,1)}, bf16[512,1536]{1,0:T(8,128)(2,1)}, u32[]{:S(2)}, u32[]{:S(2)}) %collective-permute-start.1) | collective-permute-done | bytes 1572896 | tf_op jit(solution)/shard_map/ppermute | solution.py:31
  109.6 103.3 %all-gather = s32[1,1,2048]{2,1,0:T(1,128)S(1)} all-gather(s32[1,1,512]{2,1,0:T(1,128)S(1)} %get-tuple-element.709), channel_id=2, replica_groups=mesh['dp'=2,'blk'=4,'head'=4] {'blk'}, dimensions={2}, use_global_device_ids=true | all-gather | bytes 10240 | tf_op jit(solution)/shard_map/all_gather | solution.py:161
  227.5 55.2 %all-reduce.5 = (bf16[1536]{0:T(1024)(128)(2,1)S(1)}, bf16[1536]{0:T(1024)(128)(2,1)S(1)}) all-reduce(bf16[1536]{0:T(1024)(128)(2,1)S(1)} %dynamic-update-slice, bf16[1536]{0:T(1024)(128)(2,1)S(1)} %dynamic-update-slice.1), channel_id=1, replica_groups=mesh['dp'=2,'blk'=4,'head'=4] {'dp','blk'}, use_global_device_ids=true, to_apply=%add | all-reduce | flops 3072 | bytes 12288
  330.6 80.6 %all_gather.68 = bf16[2048,2,96]{0,2,1:T(8,128)(2,1)S(1)} all-gather(bf16[512,2,96]{0,2,1:T(8,128)(2,1)S(1)} %all_to_all.213), channel_id=1, replica_groups=mesh['dp'=2,'blk'=4,'head'=4] {'blk'}, dimensions={0}, use_global_device_ids=true | all-gather | bytes 983040 | tf_op jit(solution)/shard_map/all_gather | solution.py:159
  412.1 17.3 %all_gather.69 = bf16[2048,2,96]{0,2,1:T(8,128)(2,1)S(1)} all-gather(bf16[512,2,96]{0,2,1:T(8,128)(2,1)S(1)} %all_to_all.220), channel_id=1, replica_groups=mesh['dp'=2,'blk'=4,'head'=4] {'blk'}, dimensions={0}, use_global_device_ids=true | all-gather | bytes 983040 | tf_op jit(solution)/shard_map/all_gather | solution.py:160
  431.3 18.9 %all_gather.59 = bf16[2048,2,96]{0,2,1:T(8,128)(2,1)S(1)} all-gather(bf16[512,2,96]{0,2,1:T(8,128)(2,1)S(1)} %all_to_all.199), channel_id=1, replica_groups=mesh['dp'=2,'blk'=4,'head'=4] {'blk'}, dimensions={0}, use_global_device_ids=true | all-gather | bytes 983040 | tf_op jit(solution)/shard_map/all_gather | solution.py:159
  452.1 10.7 all_gather.62
  548.8 11.4 gather_fusion
  582.2 10.5 multiply_convert_fusion.2
  597.9 11.6 multiply_reduce_fusion.1
  633.5 10.4 multiply_reduce_fusion
  668.7 54.9 %while.25 = (s32[]{:T(128)}, f32[1,512,2,2,96]{1,4,3,2,0:T(8,128)}, bf16[4,512,2,96]{1,3,2,0:T(8,128)(2,1)}, bf16[4,512,2,96]{1,3,2,0:T(8,128)(2,1)}, bf16[4,512...) while((s32[]{:T(128)}, f32[1,512,2,2,96]{1,4,3,2,0:T(8,128)}, ...), condition=%wide.region_18.19_spmd.clone, body=%wide.region_17.18_spmd.clone.sunk | while | flops 1018593792 | bytes 67217776 | solution.py:294
  730.5 51.0 %while.24 = (s32[]{:T(128)}, f32[1,512,2,2,96]{1,4,3,2,0:T(8,128)S(1)}, bf16[4,512,2,96]{1,3,2,0:T(8,128)(2,1)}, bf16[4,512,2,96]{1,3,2,0:T(8,128)(2,1)}, bf16[4...) while((s32[]{:T(128)}, ...), condition=%wide.region_11.12_spmd.clone, body=%wide.region_10.11_spmd.clone.sunk | while | flops 1018593792 | bytes 69314976 | solution.py:294
  793.9 16.7 %reduce-scatter.12.cloned.1.call-done = bf16[512,2,96]{0,2,1:T(8,128)(2,1)} async-done(((bf16[2048,2,96]{0,2,1:T(8,128)(2,1)}), bf16[512,2,96]{0,2,1:T(8,128)(2,1)}) %reduce-scatter.12.cloned.1.call-update) | async-done | bytes 196624 | tf_op jit(solution)/shard_map/reduce_scatter | solution.py:299
  829.4 10.8 reduce-scatter.18.cloned.1.call-done
  846.6 23.0 %reduce-scatter.14.cloned.1.call-done = bf16[512,2,96]{0,2,1:T(8,128)(2,1)} async-done(((bf16[2048,2,96]{0,2,1:T(8,128)(2,1)}), bf16[512,2,96]{0,2,1:T(8,128)(2,1)}) %reduce-scatter.14.cloned.1.call-update) | async-done | bytes 196624 | tf_op jit(solution)/shard_map/reduce_scatter | solution.py:302
  900.6 11.9 all-to-all-done.13
  916.3 12.9 all-to-all-done.9
  935.8 11.8 fusion.218
  947.6 14.7 add_convert_fusion.2
  962.6 12.1 fusion.219
  974.7 16.3 %add_convert_fusion.1 = bf16[1536,4096]{1,0:T(8,128)(2,1)} fusion(f32[1536,4096]{1,0:T(8,128)} %fusion.219, bf16[128,1536]{1,0:T(8,128)(2,1)S(1)} %copy-done.16, bf16[128,4096]{1,0:T(8,128)(2,1)S(1)} %copy-done.34), kind=kOutput, calls=%fused_computation.80 | convolution fusion | flops 1623195648 | bytes 39190528 | tf_op jit(solution)/shard_map/dot_general | solution.py:55
  992.1 11.9 fusion.164
  1004.1 15.5 add_convert_fusion
  1020.1 57.6 %reduce-scatter.20.cloned.1.call-done = bf16[192,1536]{1,0:T(8,128)(2,1)} async-done(((bf16[1536,1536]{1,0:T(8,128)(2,1)}), bf16[192,1536]{1,0:T(8,128)(2,1)}) %reduce-scatter.20.cloned.1.call-update) | async-done | bytes 589840 | tf_op jit(solution)/shard_map/reduce_scatter | solution.py:356
  1077.7 95.8 %reduce-scatter.28.cloned.1.call-done = bf16[192,4096]{1,0:T(8,128)(2,1)} async-done(((bf16[1536,4096]{1,0:T(8,128)(2,1)}), bf16[192,4096]{1,0:T(8,128)(2,1)}) %reduce-scatter.28.cloned.1.call-update) | async-done | bytes 1572880 | tf_op jit(solution)/shard_map/reduce_scatter | solution.py:356
  1173.5 95.8 %reduce-scatter.30.cloned.1.call-done = bf16[192,4096]{1,0:T(8,128)(2,1)} async-done(((bf16[1536,4096]{1,0:T(8,128)(2,1)}), bf16[192,4096]{1,0:T(8,128)(2,1)}) %reduce-scatter.30.cloned.1.call-update) | async-done | bytes 1572880 | tf_op jit(solution)/shard_map/reduce_scatter | solution.py:356
  1269.2 95.8 %reduce-scatter.32.cloned.1.call-done = bf16[512,1536]{1,0:T(8,128)(2,1)} async-done(((bf16[4096,1536]{1,0:T(8,128)(2,1)}), bf16[512,1536]{1,0:T(8,128)(2,1)}) %reduce-scatter.32.cloned.1.call-update) | async-done | bytes 1572880 | tf_op jit(solution)/shard_map/reduce_scatter | solution.py:356
  1389.1 14.9 all-reduce.4
  1404.2 12.2 all-reduce.6
  1420.1 179.3 %all-reduce.10.cloned.1.call-done = (bf16[192,1536]{1,0:T(8,128)(2,1)}, bf16[192,768]{1,0:T(8,128)(2,1)}, bf16[192,768]{1,0:T(8,128)(2,1)}, bf16[192,1536]{1,0:T...) async-done(((bf16[192,1536]{1,0:T(8,128)(2,1)}, bf16[192,768]{1,0:T(8,128)(2,1)}, bf16[192,768]{1,0:T(8,128)(2,1)}, ...) | async-done | bytes 6488080 | tf_op jit(solution)/shard_map/psum | solution.py:358
  (600 shorter events, 473.1 us)
Async XLA Ops:
  7.2 276.2 %all-gather.9.cloned.1.call-start = ((), (), s32[]{:S(2)}) async-start(), calls=%async_computation.27 | async-start | bytes 2654208 | tf_op jit(solution)/shard_map/all_gather | solution.py:133
  8.0 285.4 %all-gather.13.cloned.1.call-start = ((), (), s32[]{:S(2)}) async-start(), calls=%async_computation.29 | async-start | bytes 2654208 | tf_op jit(solution)/shard_map/all_gather | solution.py:134
  8.7 470.7 %all-gather.11.cloned.1.call-start = ((), (), s32[]{:S(2)}) async-start(), calls=%async_computation.28 | async-start | bytes 5308416 | tf_op jit(solution)/shard_map/all_gather | solution.py:132
  9.5 552.5 %all-gather.15.cloned.1.call-start = ((), (), s32[]{:S(2)}) async-start(), calls=%async_computation.30 | async-start | bytes 5308416 | tf_op jit(solution)/shard_map/all_gather | solution.py:135
  10.0 557.7 %all-gather.17.cloned.1.call-start = ((), (), s32[]{:S(2)}) async-start(), calls=%async_computation.31 | async-start | bytes 14155776 | tf_op jit(solution)/shard_map/all_gather | solution.py:137
  10.6 564.9 %all-gather.19.cloned.1.call-start = ((), (), s32[]{:S(2)}) async-start(), calls=%async_computation.32 | async-start | bytes 14155776 | tf_op jit(solution)/shard_map/all_gather | solution.py:138
  10.7 47.3 %collective-permute-start = (bf16[512,1536]{1,0:T(8,128)(2,1)}, bf16[512,1536]{1,0:T(8,128)(2,1)}, u32[]{:S(2)}, u32[]{:S(2)}) collective-permute-start(bf16[512,1536]{1,0:T(8,128)(2,1)} %param.27), channel_id=1, source_target_pairs={{0,4},{4,8},{8,12},{12,16},{16,20},{20,24},{24,28},{28,0},{1,5},{5... | collective-permute-start | bytes 4718600 | tf_op jit(solution)/shard_map/ppermute | solution.py:31
  58.0 48.6 %collective-permute-start.1 = (bf16[512,1536]{1,0:T(8,128)(2,1)}, bf16[512,1536]{1,0:T(8,128)(2,1)}, u32[]{:S(2)}, u32[]{:S(2)}) collective-permute-start(bf16[512,1536]{1,0:T(8,128)(2,1)} %collective-permute-done), channel_id=1, source_target_pairs={{0,4},{4,8},{8,12},{12,16},{16,20},{20,24},{24,28},{28,0},{1,5},{5... | collective-permute-start | bytes 4718600 | tf_op jit(solution)/shard_map/ppermute | solution.py:31
  59.6 164.2 %collective-permute-start.4 = (bf16[512,1536]{1,0:T(8,128)(2,1)S(1)}, bf16[512,1536]{1,0:T(8,128)(2,1)}, u32[]{:S(2)}, u32[]{:S(2)}) collective-permute-start(bf16[512,1536]{1,0:T(8,128)(2,1)S(1)} %copy-done.66), channel_id=1, source_target_pairs={{4,0},{8,4},{12,8},{16,12},{20,16},{24,20},{28,24},{0,28},{5,1},{9... | collective-permute-start | bytes 4718600 | tf_op jit(solution)/shard_map/ppermute | solution.py:34
  106.5 185.5 %collective-permute-start.2 = (bf16[512,1536]{1,0:T(8,128)(2,1)}, bf16[512,1536]{1,0:T(8,128)(2,1)}, u32[]{:S(2)}, u32[]{:S(2)}) collective-permute-start(bf16[512,1536]{1,0:T(8,128)(2,1)} %collective-permute-done.1), channel_id=1, source_target_pairs={{0,4},{4,8},{8,12},{12,16},{16,20},{20,24},{24,28},{28,0},{1,5},{5... | collective-permute-start | bytes 4718600 | tf_op jit(solution)/shard_map/ppermute | solution.py:31
  223.8 100.4 %collective-permute-start.5 = (bf16[512,1536]{1,0:T(8,128)(2,1)}, bf16[512,1536]{1,0:T(8,128)(2,1)}, u32[]{:S(2)}, u32[]{:S(2)}) collective-permute-start(bf16[512,1536]{1,0:T(8,128)(2,1)} %collective-permute-done.4), channel_id=1, source_target_pairs={{4,0},{8,4},{12,8},{16,12},{20,16},{24,20},{28,24},{0,28},{5,1},{9... | collective-permute-start | bytes 4718600 | tf_op jit(solution)/shard_map/ppermute | solution.py:34
  292.0 172.6 %collective-permute-start.3 = (bf16[512,1536]{1,0:T(8,128)(2,1)}, bf16[512,1536]{1,0:T(8,128)(2,1)}, u32[]{:S(2)}, u32[]{:S(2)}) collective-permute-start(bf16[512,1536]{1,0:T(8,128)(2,1)} %collective-permute-done.2), channel_id=1, source_target_pairs={{0,4},{4,8},{8,12},{12,16},{16,20},{20,24},{24,28},{28,0},{1,5},{5... | collective-permute-start | bytes 4718600 | tf_op jit(solution)/shard_map/ppermute | solution.py:31
  324.2 222.0 %collective-permute-start.6 = (bf16[512,1536]{1,0:T(8,128)(2,1)}, bf16[512,1536]{1,0:T(8,128)(2,1)}, u32[]{:S(2)}, u32[]{:S(2)}) collective-permute-start(bf16[512,1536]{1,0:T(8,128)(2,1)} %collective-permute-done.5), channel_id=1, source_target_pairs={{4,0},{8,4},{12,8},{16,12},{20,16},{24,20},{28,24},{0,28},{5,1},{9... | collective-permute-start | bytes 4718600 | tf_op jit(solution)/shard_map/ppermute | solution.py:34
  497.6 21.4 %all-to-all-start.1 = ((bf16[128,16,96]{0,2,1:T(8,128)(2,1)}), bf16[128,16,96]{0,2,1:T(8,128)(2,1)}, u32[]{:S(2)}, u32[]{:S(2)}) async-start(bf16[128,16,96]{0,2,1:T(8,128)(2,1)} %bitcast.9), calls=%async_computation.1 | async-start | bytes 786432 | tf_op jit(solution)/shard_map/all_to_all | solution.py:151
  519.0 22.1 %all-to-all-start.7 = ((bf16[512,4,96]{2,1,0:T(4,128)(2,1)}), bf16[512,4,96]{2,1,0:T(4,128)(2,1)S(1)}, u32[]{:S(2)}, u32[]{:S(2)}) async-start(bf16[512,4,96]{2,1,0:T(4,128)(2,1)} %copy.204), calls=%async_computation.7 | async-start | bytes 1048576 | tf_op jit(solution)/shard_map/all_to_all | solution.py:205
  541.1 20.5 %all-to-all-start.3 = ((bf16[512,4,96]{2,1,0:T(4,128)(2,1)}), bf16[512,4,96]{2,1,0:T(4,128)(2,1)S(1)}, u32[]{:S(2)}, u32[]{:S(2)}) async-start(bf16[512,4,96]{2,1,0:T(4,128)(2,1)} %copy.194), calls=%async_computation.3 | async-start | bytes 1048576 | tf_op jit(solution)/shard_map/all_to_all | solution.py:205
  660.9 65.0 %all-to-all-start.8 = ((bf16[128,16,96]{0,2,1:T(8,128)(2,1)}), bf16[128,16,96]{0,2,1:T(8,128)(2,1)}, u32[]{:S(2)}, u32[]{:S(2)}) async-start(bf16[128,16,96]{0,2,1:T(8,128)(2,1)} %bitcast.68), calls=%async_computation.8 | async-start | bytes 786432 | tf_op jit(solution)/shard_map/all_to_all | solution.py:233
  665.0 122.0 %reduce-scatter.16.cloned.1.call-start = ((), (), s32[]{:S(2)}) async-start(), calls=%async_computation.35 | async-start | bytes 983040 | tf_op jit(solution)/shard_map/reduce_scatter | solution.py:299
  725.8 84.8 %reduce-scatter.12.cloned.1.call-start = ((), (), s32[]{:S(2)}) async-start(), calls=%async_computation.33 | async-start | bytes 983040 | tf_op jit(solution)/shard_map/reduce_scatter | solution.py:299
  783.8 56.4 %reduce-scatter.18.cloned.1.call-start = ((), (), s32[]{:S(2)}) async-start(), calls=%async_computation.36 | async-start | bytes 983040 | tf_op jit(solution)/shard_map/reduce_scatter | solution.py:302
  786.0 83.6 %reduce-scatter.14.cloned.1.call-start = ((), (), s32[]{:S(2)}) async-start(), calls=%async_computation.34 | async-start | bytes 983040 | tf_op jit(solution)/shard_map/reduce_scatter | solution.py:302
  788.9 23.5 %all-to-all-start.14 = ((bf16[512,2,96]{2,1,0:T(2,128)(2,1)}), bf16[512,2,96]{2,1,0:T(2,128)(2,1)S(1)}, u32[]{:S(2)}, u32[]{:S(2)}) async-start(bf16[512,2,96]{2,1,0:T(2,128)(2,1)} %copy.232), calls=%async_computation.17 | async-start | bytes 524288 | tf_op jit(solution)/shard_map/all_to_all | solution.py:309
  817.0 202.9 %reduce-scatter.22.cloned.1.call-start = ((), (), s32[]{:S(2)}) async-start(), calls=%async_computation.38 | async-start | bytes 2654208 | tf_op jit(solution)/shard_map/reduce_scatter | solution.py:356
  842.0 29.4 %all-to-all-start.15 = ((bf16[512,2,96]{2,1,0:T(2,128)(2,1)}), bf16[512,2,96]{2,1,0:T(2,128)(2,1)S(1)}, u32[]{:S(2)}, u32[]{:S(2)}) async-start(bf16[512,2,96]{2,1,0:T(2,128)(2,1)} %copy.236), calls=%async_computation.19 | async-start | bytes 524288 | tf_op jit(solution)/shard_map/all_to_all | solution.py:312
  876.0 143.9 %reduce-scatter.24.cloned.1.call-start = ((), (), s32[]{:S(2)}) async-start(), calls=%async_computation.39 | async-start | bytes 2654208 | tf_op jit(solution)/shard_map/reduce_scatter | solution.py:356
  888.4 131.6 %reduce-scatter.26.cloned.1.call-start = ((), (), s32[]{:S(2)}) async-start(), calls=%async_computation.40 | async-start | bytes 5308416 | tf_op jit(solution)/shard_map/reduce_scatter | solution.py:356
  912.5 16.8 %all-to-all-start.9 = ((bf16[512,4,96]{2,1,0:T(4,128)(2,1)}), bf16[512,4,96]{2,1,0:T(4,128)(2,1)S(1)}, u32[]{:S(2)}, u32[]{:S(2)}) async-start(bf16[512,4,96]{2,1,0:T(4,128)(2,1)} %bitcast.73), calls=%async_computation.9 | async-start | bytes 1048576 | tf_op jit(solution)/shard_map/all_to_all | solution.py:306
  916.0 161.7 %reduce-scatter.20.cloned.1.call-start = ((), (), s32[]{:S(2)}) async-start(), calls=%async_computation.37 | async-start | bytes 5308416 | tf_op jit(solution)/shard_map/reduce_scatter | solution.py:356
  934.8 238.6 %reduce-scatter.28.cloned.1.call-start = ((), (), s32[]{:S(2)}) async-start(), calls=%async_computation.41 | async-start | bytes 14155776 | tf_op jit(solution)/shard_map/reduce_scatter | solution.py:356
  962.4 306.9 %reduce-scatter.30.cloned.1.call-start = ((), (), s32[]{:S(2)}) async-start(), calls=%async_computation.42 | async-start | bytes 14155776 | tf_op jit(solution)/shard_map/reduce_scatter | solution.py:356
  991.0 374.0 %reduce-scatter.32.cloned.1.call-start = ((), (), s32[]{:S(2)}) async-start(), calls=%async_computation.43 | async-start | bytes 14155776 | tf_op jit(solution)/shard_map/reduce_scatter | solution.py:356
  1019.6 579.8 %all-reduce.10.cloned.1.call-start = ((), (), s32[]{:S(2)}) async-start(), calls=%async_computation.44 | async-start | bytes 12976128 | tf_op jit(solution)/shard_map/psum | solution.py:358
  (150 other events, 3789.0 us)
Sparse Core Ops, SparseCore 0:
  10.0 42.2 all-gather.8
  54.1 38.4 all-gather.12
  94.5 56.7 all-gather.10
  153.1 58.6 all-gather.14
  213.5 140.7 all-gather.16
  356.1 103.1 all-gather.18
  726.0 26.6 reduce-scatter.15
  783.9 26.6 reduce-scatter.11
  814.1 26.0 reduce-scatter.17
  843.5 26.0 reduce-scatter.13
  873.6 42.4 reduce-scatter.21
  920.2 42.4 reduce-scatter.23
  966.2 53.8 reduce-scatter.25
  1023.8 53.8 reduce-scatter.19
  1081.0 92.4 reduce-scatter.27
  1176.8 92.3 reduce-scatter.29
  1272.6 92.3 reduce-scatter.31
  1367.8 231.5 all-reduce.9
